TPU v7x, 32 devices: a whole 2x2x4 slice. The times are simulated.
32 devices in a mesh: dp: 8 (over y, x, core), head: 4 (over z).
Axes of the slice: x: 2, y: 2, z: 4, core: 2. Of those that a mesh axis runs over, the one named last changes fastest.
Arguments:
- block_input: bfloat16 [8192, 1536], P(('dp', 'head')), may hold values from -6 to 6
- seq_lengths: int32 [32], P('dp'), may hold values from 1 to 256, 5120 in all
- cotangent: bfloat16 [8192, 1536], P(('dp', 'head')), may hold values from -6 to 6
- norm_gain: float32 [1536], replicated, may hold values from 0.5 to 1.5
- proj_zx: float32 [1536, 2, 3072], P('dp', None, 'head'), may hold values from -0.15625 to 0.15625
- proj_dt: float32 [1536, 48], P('dp', 'head'), may hold values from -0.15625 to 0.15625
- proj_bc: float32 [1536, 256], P('dp'), may hold values from -0.15625 to 0.15625
- chan_params: float32 [6, 3072], P(None, 'head'), may hold values from -2 to 2, as said below
- conv_bc: float32 [5, 256], replicated, may hold values from -3 to 3, as said below
- head_params: float32 [3, 48], P(None, 'head'), may hold values from -5 to 3.2, as said below
- out_proj: float32 [3072, 1536], P(('head', 'dp')), may hold values from -0.109375 to 0.109375
- gain_moments: float32 [2, 1536], replicated, may hold values from -40 to 40, as said below
- zx_moments: float32 [2, 1536, 2, 3072], P(None, 'dp', None, 'head'), may hold values from -40 to 40, as said below
- dt_moments: float32 [2, 1536, 48], P(None, 'dp', 'head'), may hold values from -40 to 40, as said below
- bc_moments: float32 [2, 1536, 256], P(None, 'dp'), may hold values from -40 to 40, as said below
- chan_moments: float32 [2, 6, 3072], P(None, None, 'head'), may hold values from -40 to 40, as said below
- convbc_moments: float32 [2, 5, 256], replicated, may hold values from -40 to 40, as said below
- head_moments: float32 [2, 3, 48], P(None, None, 'head'), may hold values from -40 to 40, as said below
- out_moments: float32 [2, 3072, 1536], P(None, ('head', 'dp')), may hold values from -40 to 40, as said below
Outputs:
- block_output: bfloat16 [8192, 1536], P(('dp', 'head'))
- input_grad: float32 [8192, 1536], P(('dp', 'head'))
- gain_next: float32 [1536], replicated
- gain_state: float32 [2, 1536], replicated
- zx_next: float32 [1536, 2, 3072], P('dp', None, 'head')
- zx_state: float32 [2, 1536, 2, 3072], P(None, 'dp', None, 'head')
- dt_next: float32 [1536, 48], P('dp', 'head')
- dt_state: float32 [2, 1536, 48], P(None, 'dp', 'head')
- bc_next: float32 [1536, 256], P('dp')
- bc_state: float32 [2, 1536, 256], P(None, 'dp')
- chan_next: float32 [6, 3072], P(None, 'head')
- chan_state: float32 [2, 6, 3072], P(None, None, 'head')
- convbc_next: float32 [5, 256], replicated
- convbc_state: float32 [2, 5, 256], replicated
- head_next: float32 [3, 48], P(None, 'head')
- head_state: float32 [2, 3, 48], P(None, None, 'head')
- outproj_next: float32 [3072, 1536], P(('head', 'dp'))
- outproj_state: float32 [2, 3072, 1536], P(None, ('head', 'dp'))
Inputs may be any that keep to these rules, and one draw needn't show every extreme that they name: Each padded sequence is live on its first seq_lengths positions; the lengths sum to 5120 and some sequence is live on all 256 positions. `chan_params`: taps in -2 to 2, bias in -0.5 to 0.5, gate gains in 0.5 to 1.5. `conv_bc`: taps and biases of B and C. `head_params`: A_log in -3 to 3.2, step bias in -5 to -1, skip coefficient in 0.5 to 1.5. `gain_moments`: root second moments lie in 3 to 40. `zx_moments`: root second moments lie in 3 to 40. `dt_moments`: root second moments lie in 3 to 40. `bc_moments`: root second moments lie in 3 to 40. `chan_moments`: root second moments lie in 3 to 40. `convbc_moments`: root second moments lie in 3 to 40. `head_moments`: root second moments lie in 3 to 40. `out_moments`: root second moments lie in 3 to 40.
All inputs are finite; a program needn't handle non-finite values. No bound on the sum of `seq_lengths` on one device may be relied on, other than what follows from the above.
Results may differ from a plain program's by a relative error of at most 0.012.
Values may be sent and summed in bfloat16 or wider, within the bound.
No kernel may reach another device: no remote copies, remote signals or barrier semaphores. Data moves between devices by JAX's collectives and lax.ppermute only.
A program may use at most 128 MiB of HBM per device.

v0:
```python
import jax
import jax.numpy as jnp
from jax import lax
from jax.sharding import PartitionSpec as P

norm_eps = 1e-05
beta_one = 0.9
beta_two = 0.95
adam_eps = 1e-08
step_count = 3.0
rate_matrix = 0.005
rate_vector = 0.2
weight_decay = 0.1
highest = lax.Precision.HIGHEST


def causal(values, tap_rows):
    kernel = tap_rows.shape[0] - 1
    length = values.shape[0]
    padded = jnp.pad(values, ((kernel - 1, 0), (0, 0)))
    summed = jnp.broadcast_to(tap_rows[kernel][None, :], values.shape)
    for offset in range(kernel):
        summed = summed + tap_rows[offset][None, :] * padded[offset : offset + length]
    return summed


def mixer_slot(proj_rows, bc_rows, step_raw, conv_taps, conv_shared, head_table):
    length = proj_rows.shape[0]
    inner_loc = conv_taps.shape[1]
    heads_loc = head_table.shape[1]
    headdim = inner_loc // heads_loc
    state_dim = bc_rows.shape[1] // 2
    gate_pre = proj_rows[:, :inner_loc]
    conv_x = jax.nn.silu(causal(proj_rows[:, inner_loc:], conv_taps))
    shared = jax.nn.silu(causal(bc_rows, conv_shared))
    input_map = shared[:, :state_dim]
    output_map = shared[:, state_dim:]
    step_size = jax.nn.softplus(step_raw + head_table[1][None, :])
    decay_rate = -jnp.exp(head_table[0])
    row_pos = lax.broadcasted_iota(jnp.int32, (length, length), 0)
    col_pos = lax.broadcasted_iota(jnp.int32, (length, length), 1)
    causal_mask = row_pos >= col_pos
    lower_ones = causal_mask.astype(jnp.float32)
    cum_log = jnp.dot(lower_ones, step_size * decay_rate[None, :], precision=highest).T
    log_gap = cum_log[:, :, None] - cum_log[:, None, :]
    decay_mat = jnp.exp(jnp.where(causal_mask[None], log_gap, -1e30))
    scores = jnp.dot(output_map, input_map.T, precision=highest)
    weights = scores[None] * decay_mat * step_size.T[:, None, :]
    head_values = conv_x.reshape(length, heads_loc, headdim)
    output = jnp.einsum("hts,shp->thp", weights, head_values, precision=highest)
    output = output + head_table[2][None, :, None] * head_values
    return output.reshape(length, inner_loc) * jax.nn.silu(gate_pre)


def adam_update(parameter, moments, gradient, learn_rate, decay_coef):
    first_mom = beta_one * moments[0] + (1.0 - beta_one) * gradient
    second_mom = beta_two * moments[1] * moments[1] + (1.0 - beta_two) * gradient * gradient
    second_root = jnp.sqrt(second_mom)
    first_hat = first_mom / (1.0 - beta_one**step_count)
    second_hat = second_mom / (1.0 - beta_two**step_count)
    updated = parameter - learn_rate * (
        first_hat / (jnp.sqrt(second_hat) + adam_eps) + decay_coef * parameter
    )
    return (updated, jnp.stack([first_mom, second_root]))


def shards(
    block_input,
    seq_lengths,
    cotangent,
    norm_gain,
    proj_zx,
    proj_dt,
    proj_bc,
    chan_params,
    conv_bc,
    head_params,
    out_proj,
    gain_moments,
    zx_moments,
    dt_moments,
    bc_moments,
    chan_moments,
    convbc_moments,
    head_moments,
    out_moments,
):
    slot_count = seq_lengths.shape[0]
    rows_own = block_input.shape[0]
    rows_dev = rows_own * lax.axis_size("head")
    seq_len = rows_dev // slot_count
    model_width = block_input.shape[1]
    inner_loc = chan_params.shape[1]
    inner_all = inner_loc * lax.axis_size("head")
    heads_loc = head_params.shape[1]
    kernel = chan_params.shape[0] - 2
    state_two = conv_bc.shape[1]
    row_start = lax.axis_index("head") * rows_own
    zx_full, dt_full, bc_full, out_full = (
        lax.all_gather(proj_zx.astype(jnp.bfloat16), "dp", axis=0, tiled=True),
        lax.all_gather(proj_dt.astype(jnp.bfloat16), "dp", axis=0, tiled=True),
        lax.all_gather(proj_bc.astype(jnp.bfloat16), "dp", axis=0, tiled=True),
        lax.all_gather(out_proj.astype(jnp.bfloat16), "dp", axis=0, tiled=True),
    )
    zx_mat = zx_full.reshape(model_width, 2 * inner_loc)
    positions = lax.broadcasted_iota(jnp.int32, (slot_count, seq_len), 1)
    live_mask = (positions < seq_lengths[:, None]).astype(jnp.float32).reshape(rows_dev, 1)
    live_own = lax.dynamic_slice_in_dim(live_mask, row_start, rows_own, 0)
    input_all = lax.all_gather(block_input, "head", axis=0, tiled=True)
    input_float = input_all.astype(jnp.float32)
    inv_norm = lax.rsqrt(jnp.mean(input_float * input_float, axis=-1, keepdims=True) + norm_eps)
    input_hat = input_float * inv_norm
    gain_float = lax.optimization_barrier(norm_gain.astype(jnp.bfloat16)).astype(jnp.float32)
    normed_in = (input_hat * gain_float[None, :]).astype(jnp.bfloat16)
    proj_out = jnp.dot(normed_in, zx_mat, preferred_element_type=jnp.float32)
    step_raw = jnp.dot(normed_in, dt_full, preferred_element_type=jnp.float32)
    bc_out = jnp.dot(normed_in, bc_full, preferred_element_type=jnp.float32)
    proj_slots = proj_out.reshape(slot_count, seq_len, 2 * inner_loc)
    bc_slots = bc_out.reshape(slot_count, seq_len, state_two)
    step_slots = step_raw.reshape(slot_count, seq_len, heads_loc)
    conv_taps = chan_params[: kernel + 1]
    gate_gain = chan_params[kernel + 1]

    def forward_slot(members_slot):
        return mixer_slot(
            members_slot[0], members_slot[1], members_slot[2], conv_taps, conv_bc, head_params
        )

    gated_rows = lax.map(forward_slot, (proj_slots, bc_slots, step_slots)).reshape(
        rows_dev, inner_loc
    )
    square_sum = lax.psum(jnp.sum(gated_rows * gated_rows, axis=-1), "head")
    inv_gate = lax.rsqrt(square_sum[:, None] / inner_all + norm_eps)
    normed_out = (gated_rows * inv_gate * gate_gain[None, :]).astype(jnp.bfloat16)
    branch = lax.psum_scatter(
        jnp.dot(normed_out, out_full, preferred_element_type=jnp.float32).astype(jnp.bfloat16),
        "head",
        scatter_dimension=0,
        tiled=True,
    ).astype(jnp.float32)
    block_output = (block_input.astype(jnp.float32) + live_own * branch).astype(jnp.bfloat16)
    cot_all = lax.all_gather(cotangent, "head", axis=0, tiled=True)
    cot_live = (cot_all.astype(jnp.float32) * live_mask).astype(jnp.bfloat16)
    grad_normed = jnp.dot(cot_live, out_full.T, preferred_element_type=jnp.float32)
    grad_out = jnp.dot(normed_out.T, cot_live, preferred_element_type=jnp.float32)
    grad_gate = jnp.sum(grad_normed * gated_rows * inv_gate, axis=0)
    scaled = grad_normed * gate_gain[None, :]
    cross_sum = lax.psum(jnp.sum(scaled * gated_rows, axis=-1), "head")
    grad_gated = inv_gate * scaled - gated_rows * inv_gate**3 * cross_sum[:, None] / inner_all

    def backward_slot(slot_totals, members_slot):
        unused, pullback = jax.vjp(
            mixer_slot,
            members_slot[0],
            members_slot[1],
            members_slot[2],
            conv_taps,
            conv_bc,
            head_params,
        )
        pieces = pullback(members_slot[3])
        return (
            (slot_totals[0] + pieces[3], slot_totals[1] + pieces[4], slot_totals[2] + pieces[5]),
            (pieces[0], pieces[1], pieces[2]),
        )

    zero_slot = (jnp.zeros_like(conv_taps), jnp.zeros_like(conv_bc), jnp.zeros_like(head_params))
    slot_grads, slot_cots = lax.scan(
        backward_slot,
        zero_slot,
        (proj_slots, bc_slots, step_slots, grad_gated.reshape(slot_count, seq_len, inner_loc)),
    )
    cot_proj = slot_cots[0].reshape(rows_dev, 2 * inner_loc).astype(jnp.bfloat16)
    cot_bc = slot_cots[1].reshape(rows_dev, state_two).astype(jnp.bfloat16)
    cot_step = slot_cots[2].reshape(rows_dev, heads_loc).astype(jnp.bfloat16)
    cot_input = jnp.dot(cot_proj, zx_mat.T, preferred_element_type=jnp.float32)
    cot_input = cot_input + jnp.dot(cot_step, dt_full.T, preferred_element_type=jnp.float32)
    cot_input = cot_input + jnp.dot(cot_bc, bc_full.T, preferred_element_type=jnp.float32)
    grad_zx = jnp.dot(normed_in.T, cot_proj, preferred_element_type=jnp.float32).reshape(
        model_width, 2, inner_loc
    )
    grad_dt = jnp.dot(normed_in.T, cot_step, preferred_element_type=jnp.float32)
    grad_bc = jnp.dot(normed_in.T, cot_bc, preferred_element_type=jnp.float32)
    inv_own = lax.dynamic_slice_in_dim(inv_norm, row_start, rows_own, 0)
    own_hat = block_input.astype(jnp.float32) * inv_own
    cot_whole = lax.psum(cot_input.astype(jnp.bfloat16), "head").astype(jnp.float32)
    row_dot = jnp.sum(cot_whole * gain_float[None, :] * input_hat, axis=-1, keepdims=True)
    cot_own = lax.dynamic_slice_in_dim(cot_whole, row_start, rows_own, 0)
    row_own = lax.dynamic_slice_in_dim(row_dot, row_start, rows_own, 0)
    input_grad = cotangent.astype(jnp.float32) + inv_own * (
        cot_own * gain_float[None, :] - own_hat * row_own / model_width
    )
    grad_gain = jnp.sum(cot_own * own_hat, axis=0)
    grad_zx, grad_dt, grad_bc, grad_out = (
        lax.psum_scatter(
            grad_zx.astype(jnp.bfloat16), "dp", scatter_dimension=0, tiled=True
        ).astype(jnp.float32),
        lax.psum_scatter(
            grad_dt.astype(jnp.bfloat16), "dp", scatter_dimension=0, tiled=True
        ).astype(jnp.float32),
        lax.psum_scatter(
            grad_bc.astype(jnp.bfloat16), "dp", scatter_dimension=0, tiled=True
        ).astype(jnp.float32),
        lax.psum_scatter(
            grad_out.astype(jnp.bfloat16), "dp", scatter_dimension=0, tiled=True
        ).astype(jnp.float32),
    )
    grad_chan = jnp.concatenate([slot_grads[0], grad_gate[None, :]], axis=0)
    grad_gain, grad_chan, grad_head, grad_convbc = lax.psum(
        (grad_gain, grad_chan, slot_grads[2], slot_grads[1]), "dp"
    )
    grad_bc, grad_convbc, grad_gain = (
        lax.psum(grad_bc.astype(jnp.bfloat16), "head").astype(jnp.float32),
        lax.psum(grad_convbc.astype(jnp.bfloat16), "head").astype(jnp.float32),
        lax.psum(grad_gain.astype(jnp.bfloat16), "head").astype(jnp.float32),
    )
    gain_next, gain_state = adam_update(norm_gain, gain_moments, grad_gain, rate_vector, 0.0)
    zx_next, zx_state = adam_update(proj_zx, zx_moments, grad_zx, rate_matrix, weight_decay)
    dt_next, dt_state = adam_update(proj_dt, dt_moments, grad_dt, rate_matrix, weight_decay)
    bc_next, bc_state = adam_update(proj_bc, bc_moments, grad_bc, rate_matrix, weight_decay)
    chan_next, chan_state = adam_update(chan_params, chan_moments, grad_chan, rate_vector, 0.0)
    convbc_next, convbc_state = adam_update(conv_bc, convbc_moments, grad_convbc, rate_vector, 0.0)
    head_next, head_state = adam_update(head_params, head_moments, grad_head, rate_vector, 0.0)
    outproj_next, outproj_state = adam_update(
        out_proj, out_moments, grad_out, rate_matrix, weight_decay
    )
    return (
        block_output,
        input_grad,
        gain_next,
        gain_state,
        zx_next,
        zx_state,
        dt_next,
        dt_state,
        bc_next,
        bc_state,
        chan_next,
        chan_state,
        convbc_next,
        convbc_state,
        head_next,
        head_state,
        outproj_next,
        outproj_state,
    )


def solution(mesh):
    placed = (
        P(("dp", "head"), None),
        P("dp"),
        P(("dp", "head"), None),
        P(),
        P("dp", None, "head"),
        P("dp", "head"),
        P("dp", None),
        P(None, "head"),
        P(),
        P(None, "head"),
        P(("head", "dp"), None),
        P(),
        P(None, "dp", None, "head"),
        P(None, "dp", "head"),
        P(None, "dp", None),
        P(None, None, "head"),
        P(),
        P(None, None, "head"),
        P(None, ("head", "dp"), None),
    )
    return jax.shard_map(
        shards,
        mesh=mesh,
        in_specs=placed,
        out_specs=(
            P(("dp", "head"), None),
            P(("dp", "head"), None),
            P(),
            P(),
            P("dp", None, "head"),
            P(None, "dp", None, "head"),
            P("dp", "head"),
            P(None, "dp", "head"),
            P("dp", None),
            P(None, "dp", None),
            P(None, "head"),
            P(None, None, "head"),
            P(),
            P(),
            P(None, "head"),
            P(None, None, "head"),
            P(("head", "dp"), None),
            P(None, ("head", "dp"), None),
        ),
        check_vma=False,
    )
```

profile of v0, /device:TPU:0, one launch (start us, length us, event | category | flops | bytes accessed | tf_op | source)
XLA Modules:
  0.0 714.8 jit_solution(882251160323522166)
XLA Ops:
  12.2 12.9 %all_gather.20 = bf16[1536,256]{1,0:T(8,128)(2,1)} all-gather(bf16[192,256]{1,0:T(8,128)(2,1)S(1)} %convert_element_type.153), channel_id=1, replica_groups=mesh['dp'=8,'head'=4] {'dp'}, dimensions={0}, use_global_device_ids=true | all-gather | bytes 884736 | tf_op jit(solution)/shard_map/all_gather | solution.py:102
  25.1 9.1 %all-gather = bf16[8,192,12]{1,2,0:T(8,128)(2,1)S(1)} all-gather(bf16[1,192,12]{1,2,0:T(8,128)(2,1)S(1)} %convert_bitcast_fusion), channel_id=1, replica_groups=mesh['dp'=8,'head'=4] {'dp'}, dimensions={0}, use_global_device_ids=true | all-gather | bytes 41472 | tf_op jit(solution)/shard_map/all_gather | solution.py:101
  35.1 40.8 %all-gather.6.cloned.1.call-done = bf16[1024,1536]{1,0:T(8,128)(2,1)} async-done(((bf16[256,1536]{1,0:T(8,128)(2,1)}), bf16[1024,1536]{1,0:T(8,128)(2,1)}) %all-gather.6.cloned.1.call-update) | async-done | bytes 3145744 | tf_op jit(solution)/shard_map/all_gather | solution.py:109
  82.8 33.0 %all-gather.8.cloned.1.call-done = bf16[1536,2,768]{2,1,0:T(2,128)(2,1)} async-done(((bf16[192,2,768]{2,1,0:T(2,128)(2,1)}), bf16[1536,2,768]{2,1,0:T(2,128)(2,1)}) %all-gather.8.cloned.1.call-update) | async-done | bytes 4718608 | tf_op jit(solution)/shard_map/all_gather | solution.py:100
  115.8 11.4 %reshape.322 = bf16[1536,1536,1]{1,0,2:T(8,128)(2,1)} reshape(bf16[1536,2,768]{2,1,0:T(2,128)(2,1)} %all-gather.8.cloned.1.call-done) | data formatting | bytes 9437184 | tf_op jit(solution)/shard_map/reshape | solution.py:105
  127.2 9.4 %fusion.160 = f32[4,256,1536]{1,2,0:T(8,128)} fusion(bf16[4,256,1536]{2,1,0:T(8,128)(2,1)S(1)} %bitcast.438, bf16[1536,1536,1]{1,0,2:T(8,128)(2,1)} %reshape.322), kind=kOutput, calls=%fused_computation.316 | convolution fusion | flops 4831838208 | bytes 14155776 | tf_op jit(solution)/shard_map/dot_general | solution.py:115
  136.6 39.3 %while.36 = (s32[]{:T(128)}, f32[4,256,768]{1,2,0:T(8,128)}, f32[5,768]{1,0:T(8,128)S(1)}, f32[4,256,1536]{1,2,0:T(8,128)}, f32[5,256]{1,0:T(8,128)S(1)}, /*inde...) while((s32[]{:T(128)}, f32[4,256,768]{1,2,0:T(8,128)}, ...), condition=%wide.region_2.3_spmd, body=%wide.region_1.2_spmd.sunk | while | flops 721925120 | bytes 12330901 | solution.py:129
  179.9 12.4 %psum.70 = f32[1024]{0:T(1024)S(1)} all-reduce(f32[1024]{0:T(1024)S(1)} %bitcast.479), channel_id=1, replica_groups=mesh['dp'=8,'head'=4] {'head'}, use_global_device_ids=true, to_apply=%region_4.5 | all-reduce | flops 1024 | bytes 8192 | tf_op jit(solution)/shard_map/psum | solution.py:132
  192.3 20.0 %all-gather.12.cloned.1.call-done = bf16[1024,1536]{1,0:T(8,128)(2,1)} async-done(((bf16[256,1536]{1,0:T(8,128)(2,1)}), bf16[1024,1536]{1,0:T(8,128)(2,1)}) %all-gather.12.cloned.1.call-update) | async-done | bytes 3145744 | tf_op jit(solution)/shard_map/all_gather | solution.py:142
  212.3 8.8 %fusion.111 = (f32[768]{0:T(1024)}, f32[1024]{0:T(1024)S(1)}, f32[1024,768]{1,0:T(8,128)}) fusion(f32[4,256,768]{2,1,0:T(8,128)} %copy.117, f32[1024]{0:T(1024)S(1)} %get-tuple-element.747, f32[768]{0:T(1024)S(1)} %slice_reduce_fusion.11, bf16[768,1536]{1,0:T(8,128)(2,1)} %all-gather.10.cloned.1.call-done, ...), kind=kOutput, calls=%fused_computation.196 | convolution fusion | flops 2425354496 | bytes 11814912 | tf_op jit(solution)/shard_map/dot_general | solution.py:144
  221.1 9.0 %psum.71 = f32[1024]{0:T(1024)S(1)} all-reduce(f32[1024]{0:T(1024)S(1)} %get-tuple-element.611), channel_id=1, replica_groups=mesh['dp'=8,'head'=4] {'head'}, use_global_device_ids=true, to_apply=%region_7.8 | all-reduce | flops 1024 | bytes 8192 | tf_op jit(solution)/shard_map/psum | solution.py:148
  234.3 98.4 %while.37 = (s32[]{:T(128)}, f32[5,768]{1,0:T(8,128)S(1)}, f32[5,256]{1,0:T(8,128)S(1)}, f32[3,12]{1,0:T(4,128)S(1)}, bf16[4,256,1536]{2,1,0:T(8,128)(2,1)}, /*i...) while((s32[]{:T(128)}, f32[5,768]{1,0:T(8,128)S(1)}, ...), condition=%wide.region_27.28_spmd.clone, body=%wide.region_8.27_spmd.clone.sunk | while | flops 2164275456 | bytes 51899236 | solution.py:168
  338.6 6.6 convolution_convert_fusion.2
  358.3 12.6 %reduce-scatter.12.cloned.1.call-done = bf16[192,256]{1,0:T(8,128)(2,1)} async-done(((bf16[1536,256]{1,0:T(8,128)(2,1)}), bf16[192,256]{1,0:T(8,128)(2,1)}) %reduce-scatter.12.cloned.1.call-update) | async-done | bytes 98320 | tf_op jit(solution)/shard_map/reduce_scatter | solution.py:201
  371.0 6.4 convolution_convert_fusion.1
  382.3 8.8 %convolution_convert_fusion = bf16[1536,2,768]{2,0,1:T(8,128)(2,1)} fusion(bf16[2,768,1024]{2,1,0:T(8,128)(2,1)} %bitcast.448, bf16[1024,1536]{1,0:T(8,128)(2,1)S(1)} %copy-done.1), kind=kOutput, calls=%fused_computation.181 | convolution fusion | flops 4834197504 | bytes 11010048 | tf_op jit(solution)/shard_map/dot_general | solution.py:179
  399.3 9.0 %reduce-scatter.16.cloned.1.call-done = bf16[192,12]{1,0:T(8,128)(2,1)} async-done(((bf16[1536,12]{1,0:T(8,128)(2,1)}), bf16[192,12]{1,0:T(8,128)(2,1)}) %reduce-scatter.16.cloned.1.call-update) | async-done | bytes 4624
  410.5 44.1 %reduce-scatter.14.cloned.1.call-done = bf16[96,1536]{1,0:T(8,128)(2,1)} async-done(((bf16[768,1536]{1,0:T(8,128)(2,1)}), bf16[96,1536]{1,0:T(8,128)(2,1)}) %reduce-scatter.14.cloned.1.call-update) | async-done | bytes 294928 | tf_op jit(solution)/shard_map/reduce_scatter | solution.py:204
  458.5 122.8 %all-reduce.34.cloned.1.call-done = (bf16[1024,1536]{1,0:T(8,128)(2,1)}, bf16[192,256]{1,0:T(8,128)(2,1)}) async-done(((bf16[1024,1536]{1,0:T(8,128)(2,1)}, bf16[192,256]{1,0:T(8,128)(2,1)}), (bf16[1024,1536]{1,0:T(8,128)(2,1)}, bf16[192,256]{1,0:T(8,128)(2,1)})) %all-reduce.34.cloned.1.call-update) | async-done | bytes 3244048 | tf_op jit(solution)/shard_map/psum | solution.py:186
  581.3 5.6 convert_element_type.172
  590.6 52.5 %reduce-scatter.8.cloned.1.call-done = bf16[256,1536]{1,0:T(8,128)(2,1)} async-done(((bf16[1024,1536]{1,0:T(8,128)(2,1)}), bf16[256,1536]{1,0:T(8,128)(2,1)}) %reduce-scatter.8.cloned.1.call-update) | async-done | bytes 786448 | tf_op jit(solution)/shard_map/reduce_scatter | solution.py:135
  648.0 25.3 %all-reduce.29 = (bf16[1536]{0:T(1024)(128)(2,1)}, f32[6,768]{1,0:T(8,128)}, bf16[5,256]{1,0:T(8,128)(2,1)}, f32[3,12]{1,0:T(4,128)}) all-reduce(f32[1536]{0:T(1024)} %get-tuple-element.712, f32[6,768]{1,0:T(8,128)} %pad_maximum_fusion.5, f32[5,256]{1,0:T(8,128)S(1)} %get-tuple-element.358, ...), channel_id=1, replica_groups=mesh['dp'=8,'head'=4] {'dp'}, use_global_device_ids=true, to_apply=%region_31.32 | all-reduce | flops 7460 | bytes 54048 | tf_op jit(solution)/shard_map/psum | solution.py:209
  675.2 11.6 %all-reduce.30 = (bf16[1536]{0:T(1024)(128)(2,1)S(1)}, bf16[5,256]{1,0:T(8,128)(2,1)S(1)}) all-reduce(bf16[1536]{0:T(1024)(128)(2,1)} %get-tuple-element.664, bf16[5,256]{1,0:T(8,128)(2,1)} %get-tuple-element.666), channel_id=1, replica_groups=mesh['dp'=8,'head'=4] {'head'}, use_global_device_ids=true, to_apply=%region_32.33 | all-reduce | flops 2816 | bytes 11264 | tf_op jit(solution)/shard_map/psum | solution.py:215
  692.8 7.3 %reduce-scatter.10.cloned.1.call-done = bf16[192,2,768]{2,0,1:T(8,128)(2,1)} async-done(((bf16[1536,2,768]{2,0,1:T(8,128)(2,1)}), bf16[192,2,768]{2,0,1:T(8,128)(2,1)}) %reduce-scatter.10.cloned.1.call-update) | async-done | bytes 589840 | tf_op jit(solution)/shard_map/reduce_scatter | solution.py:195
  (424 shorter events, 218.5 us)
Async XLA Ops:
  7.2 17.9 %copy-start.30 = (f32[192,12]{0,1:T(8,128)S(1)}, f32[192,12]{0,1:T(8,128)}, u32[]{:S(2)}) copy-start(f32[192,12]{0,1:T(8,128)} %param.28) | copy-start | bytes 27652
  7.2 27.1 %copy-start.27 = (f32[3,12]{1,0:T(4,128)S(1)}, f32[3,12]{1,0:T(4,128)}, u32[]{:S(2)}) copy-start(f32[3,12]{1,0:T(4,128)} %param.32) | copy-start | bytes 436
  7.2 27.1 %copy-start.42 = (s32[4]{0:T(128)S(1)}, s32[4]{0:T(128)}, u32[]{:S(2)}) copy-start(s32[4]{0:T(128)} %param.24) | copy-start | bytes 52
  7.3 27.8 %copy-start.13 = (f32[6,768]{1,0:T(8,128)S(1)}, f32[6,768]{1,0:T(8,128)}, u32[]{:S(2)}) copy-start(f32[6,768]{1,0:T(8,128)} %param.30) | copy-start | bytes 55300
  7.3 68.6 %all-gather.6.cloned.1.call-start = ((), (), s32[]{:S(2)}) async-start(), calls=%async_computation.5 | async-start | bytes 3932160 | tf_op jit(solution)/shard_map/all_gather | solution.py:109
  8.0 107.8 %all-gather.8.cloned.1.call-start = ((), (), s32[]{:S(2)}) async-start(), calls=%async_computation.6 | async-start | bytes 5308416 | tf_op jit(solution)/shard_map/all_gather | solution.py:100
  10.6 181.7 %all-gather.10.cloned.1.call-start = ((), (), s32[]{:S(2)}) async-start(), calls=%async_computation.7 | async-start | bytes 2654208 | tf_op jit(solution)/shard_map/all_gather | solution.py:103
  11.4 200.9 %all-gather.12.cloned.1.call-start = ((), (), s32[]{:S(2)}) async-start(), calls=%async_computation.9 | async-start | bytes 3932160 | tf_op jit(solution)/shard_map/all_gather | solution.py:142
  12.0 358.9 %reduce-scatter.12.cloned.1.call-start = ((), (), s32[]{:S(2)}) async-start(), calls=%async_computation.11 | async-start | bytes 884736 | tf_op jit(solution)/shard_map/reduce_scatter | solution.py:201
  12.1 67.4 %copy-start.24 = (f32[1536]{0:T(1024)}, f32[1536]{0:T(1024)S(1)}, u32[]{:S(2)}) copy-start(f32[1536]{0:T(1024)S(1)} %convert_element_type.150) | copy-start | bytes 18436
  79.8 47.4 %copy-start = (bf16[1024,1536]{1,0:T(8,128)(2,1)}, bf16[1024,1536]{1,0:T(8,128)(2,1)S(1)}, u32[]{:S(2)}) copy-start(bf16[1024,1536]{1,0:T(8,128)(2,1)S(1)} %fusion.100) | copy-start | bytes 9437188
  127.2 9.4 %copy-start.22 = (f32[5,256]{1,0:T(8,128)S(1)}, f32[5,256]{1,0:T(8,128)}, u32[]{:S(2)}) copy-start(f32[5,256]{1,0:T(8,128)} %param.31) | copy-start | bytes 15364
  212.3 17.8 %copy-start.6 = (f32[4,256,768]{2,1,0:T(8,128)S(1)}, f32[4,256,768]{2,1,0:T(8,128)}, u32[]{:S(2)}) copy-start(f32[4,256,768]{2,1,0:T(8,128)} %copy.117) | copy-start | bytes 9437188
  250.7 5.6 copy-start.20
  336.9 71.4 %reduce-scatter.16.cloned.1.call-start = ((), (), s32[]{:S(2)}) async-start(), calls=%async_computation.13 | async-start | bytes 442368
  338.5 116.1 %reduce-scatter.14.cloned.1.call-start = ((), (), s32[]{:S(2)}) async-start(), calls=%async_computation.12 | async-start | bytes 2654208 | tf_op jit(solution)/shard_map/reduce_scatter | solution.py:204
  345.2 236.1 %all-reduce.34.cloned.1.call-start = ((), (), s32[]{:S(2)}) async-start(), calls=%async_computation.14 | async-start | bytes 6488064 | tf_op jit(solution)/shard_map/psum | solution.py:186
  370.9 272.2 %reduce-scatter.8.cloned.1.call-start = ((), (), s32[]{:S(2)}) async-start(), calls=%async_computation.8 | async-start | bytes 3932160 | tf_op jit(solution)/shard_map/reduce_scatter | solution.py:135
  377.4 322.7 %reduce-scatter.10.cloned.1.call-start = ((), (), s32[]{:S(2)}) async-start(), calls=%async_computation.10 | async-start | bytes 5308416 | tf_op jit(solution)/shard_map/reduce_scatter | solution.py:195
  391.2 7.5 %copy-start.40 = (f32[768]{0:T(1024)S(1)}, f32[768]{0:T(1024)}, u32[]{:S(2)}) copy-start(f32[768]{0:T(1024)} %get-tuple-element.610) | copy-start | bytes 9220
  391.2 7.5 %copy-start.16 = (f32[5,768]{1,0:T(8,128)S(1)}, f32[5,768]{1,0:T(8,128)}, u32[]{:S(2)}) copy-start(f32[5,768]{1,0:T(8,128)} %copy-done.15) | copy-start | bytes 46084
  391.2 18.0 %copy-start.31 = (f32[192,12]{0,1:T(8,128)S(1)}, f32[192,12]{0,1:T(8,128)}, u32[]{:S(2)}) copy-start(f32[192,12]{0,1:T(8,128)} %param.28) | copy-start | bytes 27652
  391.2 63.4 %copy-start.12 = (f32[96,1536]{1,0:T(8,128)S(1)}, f32[96,1536]{1,0:T(8,128)}, u32[]{:S(2)}) copy-start(f32[96,1536]{1,0:T(8,128)} %param.33) | copy-start | bytes 1769476
  643.1 57.0 %copy-start.7 = (f32[192,2,768]{2,1,0:T(2,128)S(1)}, f32[192,2,768]{2,1,0:T(2,128)}, u32[]{:S(2)}) copy-start(f32[192,2,768]{2,1,0:T(2,128)} %param.27) | copy-start | bytes 3538948
  (35 other events, 117.4 us)
Sparse Core Ops, SparseCore 0:
  9.6 66.1 all-gather.5
  78.3 37.4 all-gather.7
  118.2 28.8 all-gather.9
  148.6 63.6 all-gather.11
  337.0 33.8 reduce-scatter.11
  374.4 33.8 reduce-scatter.15
  412.2 42.3 reduce-scatter.13
  457.0 124.2 all-reduce.33
  583.6 59.4 reduce-scatter.7
  646.4 53.6 reduce-scatter.9
where the time goes:
time: 721 us; the launch traced here: 715 us
  waiting for transfers between devices  343 us (48%)
  matrix products  125 us (17%)
  blocking collectives  80.3 us (11%)
  other arithmetic  75.3 us (10%)
  local copies, waits for them, and re-layouts  73.4 us (10%)
  between operations  15 us (2%)
    psum x1, waiting for transfers between devices, shards(): lax.psum(cot_input.astype(jnp.bfloat16), 'head').astype(jnp.float32)  123 us
    dot_general x16, matrix products, mixer_slot(): output = jnp.einsum('hts,shp->thp', weights, head_values, precision=highest)  59.5 us
    reduce_scatter x1, waiting for transfers between devices, shards(): lax.psum_scatter(jnp.dot(normed_out, out_full, preferred_element_type=jnp...  52.5 us
    reduce_scatter x1, waiting for transfers between devices, shards(): lax.psum_scatter(grad_out.astype(jnp.bfloat16), 'dp', scatter_dimension=0...  44.1 us
    all_gather x1, waiting for transfers between devices, shards(): input_all = lax.all_gather(block_input, 'head', axis=0, tiled=True)  40.8 us
    all_gather x1, waiting for transfers between devices, shards(): lax.all_gather(proj_zx.astype(jnp.bfloat16), 'dp', axis=0, tiled=True)  33 us
    psum x1, blocking collectives, shards(): lax.psum((grad_gain, grad_chan, slot_grads[2], slot_grads[1]), 'dp')  25.3 us
    squeeze x16, local copies, waits for them, and re-layouts, shards(): lax.map(forward_slot, (proj_slots, bc_slots, step_slots))  20.2 us
  transfers between devices with their start and end apart: 10, of which 9 were waited for; matrix products, arithmetic and copies ran while one was open for 21% of the time, Pallas kernels for 0%

commit v1 on v0

--- a/solution.py
+++ b/solution.py
@@ -183,7 +183,9 @@
     grad_bc = jnp.dot(normed_in.T, cot_bc, preferred_element_type=jnp.float32)
     inv_own = lax.dynamic_slice_in_dim(inv_norm, row_start, rows_own, 0)
     own_hat = block_input.astype(jnp.float32) * inv_own
-    cot_whole = lax.psum(cot_input.astype(jnp.bfloat16), "head").astype(jnp.float32)
+    cot_whole = jnp.sum(
+        lax.all_gather(cot_input.astype(jnp.bfloat16), axis_name="head"), axis=0
+    ).astype(jnp.float32)
     row_dot = jnp.sum(cot_whole * gain_float[None, :] * input_hat, axis=-1, keepdims=True)
     cot_own = lax.dynamic_slice_in_dim(cot_whole, row_start, rows_own, 0)
     row_own = lax.dynamic_slice_in_dim(row_dot, row_start, rows_own, 0)

time: 721 us -> 886 us (1.23)
  waiting for transfers between devices: 343 us -> 507 us
    all_gather x0 -> x1, waiting for transfers between devices: none -> 212 us  [shards(): lax.all_gather(cot_input.astype(jnp.bfloat16), axis_name='head')]
    psum x1, waiting for transfers between devices: 123 us -> 23.4 us  [shards(): lax.psum(grad_bc.astype(jnp.bfloat16), 'head').astype(jnp.float32)]
    reduce_scatter x1, waiting for transfers between devices: 7.3 us -> 53.2 us  [shards(): lax.psum_scatter(grad_zx.astype(jnp.bfloat16), 'dp', scatter_dimension=0,...]
    reduce_scatter x1, waiting for transfers between devices: 12.6 us -> 32.3 us  [shards(): lax.psum_scatter(grad_bc.astype(jnp.bfloat16), 'dp', scatter_dimension=0,...]
    unnamed x11 -> x12, waiting for transfers between devices: 10.4 us -> 1.35 us
  transfers between devices with their start and end apart: 10 -> 11, of which waited for: 9 -> 9; matrix products, arithmetic and copies ran while one was open for 21% -> 17% of each run, Pallas kernels for 0% -> 0%
where the time goes in v1:
time: 886 us; the launch traced here: 880 us
  waiting for transfers between devices  507 us (57%)
  matrix products  124 us (14%)
  other arithmetic  79.4 us (9%)
  blocking collectives  78.6 us (9%)
  local copies, waits for them, and re-layouts  73.9 us (8%)
  between operations  14.9 us (2%)
    all_gather x1, waiting for transfers between devices, shards(): lax.all_gather(cot_input.astype(jnp.bfloat16), axis_name='head')  212 us
    dot_general x16, matrix products, mixer_slot(): output = jnp.einsum('hts,shp->thp', weights, head_values, precision=highest)  59.5 us
    reduce_scatter x1, waiting for transfers between devices, shards(): lax.psum_scatter(grad_zx.astype(jnp.bfloat16), 'dp', scatter_dimension=0,...  53.2 us
    reduce_scatter x1, waiting for transfers between devices, shards(): lax.psum_scatter(jnp.dot(normed_out, out_full, preferred_element_type=jnp...  47.2 us
    reduce_scatter x1, waiting for transfers between devices, shards(): lax.psum_scatter(grad_out.astype(jnp.bfloat16), 'dp', scatter_dimension=0...  43.5 us
    all_gather x1, waiting for transfers between devices, shards(): input_all = lax.all_gather(block_input, 'head', axis=0, tiled=True)  40.7 us
    all_gather x1, waiting for transfers between devices, shards(): lax.all_gather(proj_zx.astype(jnp.bfloat16), 'dp', axis=0, tiled=True)  33 us
    reduce_scatter x1, waiting for transfers between devices, shards(): lax.psum_scatter(grad_bc.astype(jnp.bfloat16), 'dp', scatter_dimension=0,...  32.3 us
  transfers between devices with their start and end apart: 11, of which 9 were waited for; matrix products, arithmetic and copies ran while one was open for 17% of the time, Pallas kernels for 0%

profile of v1, /device:TPU:0, one launch (start us, length us, event | category | flops | bytes accessed | tf_op | source)
XLA Modules:
  0.0 880.1 jit_solution(1575022422675598000)
XLA Ops:
  12.2 12.9 %all_gather.26 = bf16[1536,256]{1,0:T(8,128)(2,1)} all-gather(bf16[192,256]{1,0:T(8,128)(2,1)S(1)} %convert_element_type.155), channel_id=1, replica_groups=mesh['dp'=8,'head'=4] {'dp'}, dimensions={0}, use_global_device_ids=true | all-gather | bytes 884736 | tf_op jit(solution)/shard_map/all_gather | solution.py:102
  25.1 9.1 %all-gather.1 = bf16[8,192,12]{1,2,0:T(8,128)(2,1)S(1)} all-gather(bf16[1,192,12]{1,2,0:T(8,128)(2,1)S(1)} %convert_bitcast_fusion), channel_id=1, replica_groups=mesh['dp'=8,'head'=4] {'dp'}, dimensions={0}, use_global_device_ids=true | all-gather | bytes 41472 | tf_op jit(solution)/shard_map/all_gather | solution.py:101
  35.1 40.7 %all-gather.8.cloned.1.call-done = bf16[1024,1536]{1,0:T(8,128)(2,1)} async-done(((bf16[256,1536]{1,0:T(8,128)(2,1)}), bf16[1024,1536]{1,0:T(8,128)(2,1)}) %all-gather.8.cloned.1.call-update) | async-done | bytes 3145744 | tf_op jit(solution)/shard_map/all_gather | solution.py:109
  82.8 33.0 %all-gather.10.cloned.1.call-done = bf16[1536,2,768]{2,1,0:T(2,128)(2,1)} async-done(((bf16[192,2,768]{2,1,0:T(2,128)(2,1)}), bf16[1536,2,768]{2,1,0:T(2,128)(2,1)}) %all-gather.10.cloned.1.call-update) | async-done | bytes 4718608 | tf_op jit(solution)/shard_map/all_gather | solution.py:100
  115.8 11.4 %reshape.323 = bf16[1536,1536,1]{1,0,2:T(8,128)(2,1)} reshape(bf16[1536,2,768]{2,1,0:T(2,128)(2,1)} %all-gather.10.cloned.1.call-done) | data formatting | bytes 9437184 | tf_op jit(solution)/shard_map/reshape | solution.py:105
  127.2 9.4 %fusion.160 = f32[4,256,1536]{1,2,0:T(8,128)} fusion(bf16[4,256,1536]{2,1,0:T(8,128)(2,1)S(1)} %bitcast.439, bf16[1536,1536,1]{1,0,2:T(8,128)(2,1)} %reshape.323), kind=kOutput, calls=%fused_computation.316 | convolution fusion | flops 4831838208 | bytes 14155776 | tf_op jit(solution)/shard_map/dot_general | solution.py:115
  136.6 39.2 %while.36 = (s32[]{:T(128)}, f32[4,256,768]{1,2,0:T(8,128)}, f32[5,768]{1,0:T(8,128)S(1)}, f32[4,256,1536]{1,2,0:T(8,128)}, f32[5,256]{1,0:T(8,128)S(1)}, /*inde...) while((s32[]{:T(128)}, f32[4,256,768]{1,2,0:T(8,128)}, ...), condition=%wide.region_2.3_spmd, body=%wide.region_1.2_spmd.sunk | while | flops 721925120 | bytes 12330901 | solution.py:129
  179.8 12.4 %psum.63 = f32[1024]{0:T(1024)S(1)} all-reduce(f32[1024]{0:T(1024)S(1)} %bitcast.481), channel_id=1, replica_groups=mesh['dp'=8,'head'=4] {'head'}, use_global_device_ids=true, to_apply=%region_4.5 | all-reduce | flops 1024 | bytes 8192 | tf_op jit(solution)/shard_map/psum | solution.py:132
  192.3 20.0 %all-gather.14.cloned.1.call-done = bf16[1024,1536]{1,0:T(8,128)(2,1)} async-done(((bf16[256,1536]{1,0:T(8,128)(2,1)}), bf16[1024,1536]{1,0:T(8,128)(2,1)}) %all-gather.14.cloned.1.call-update) | async-done | bytes 3145744 | tf_op jit(solution)/shard_map/all_gather | solution.py:142
  212.3 8.7 fusion.111
  221.0 9.0 %psum.64 = f32[1024]{0:T(1024)S(1)} all-reduce(f32[1024]{0:T(1024)S(1)} %get-tuple-element.611), channel_id=1, replica_groups=mesh['dp'=8,'head'=4] {'head'}, use_global_device_ids=true, to_apply=%region_7.8 | all-reduce | flops 1024 | bytes 8192 | tf_op jit(solution)/shard_map/psum | solution.py:148
  234.2 98.4 %while.37 = (s32[]{:T(128)}, f32[5,768]{1,0:T(8,128)S(1)}, f32[5,256]{1,0:T(8,128)S(1)}, f32[3,12]{1,0:T(4,128)S(1)}, bf16[4,256,1536]{2,1,0:T(8,128)(2,1)}, /*i...) while((s32[]{:T(128)}, f32[5,768]{1,0:T(8,128)S(1)}, ...), condition=%wide.region_27.28_spmd.clone, body=%wide.region_8.27_spmd.clone.sunk | while | flops 2164275456 | bytes 51899236 | solution.py:168
  338.4 32.3 %reduce-scatter.12.cloned.1.call-done = bf16[192,256]{1,0:T(8,128)(2,1)} async-done(((bf16[1536,256]{1,0:T(8,128)(2,1)}), bf16[192,256]{1,0:T(8,128)(2,1)}) %reduce-scatter.12.cloned.1.call-update) | async-done | bytes 98320 | tf_op jit(solution)/shard_map/reduce_scatter | solution.py:203
  370.8 6.6 convolution_convert_fusion.2
  382.1 8.7 convolution_convert_fusion
  405.4 5.8 convolution_convert_fusion.1
  421.6 23.4 %all-reduce.33.cloned.1.call-done = bf16[192,256]{1,0:T(8,128)(2,1)} async-done(((bf16[192,256]{1,0:T(8,128)(2,1)}), bf16[192,256]{1,0:T(8,128)(2,1)}) %all-reduce.33.cloned.1.call-update) | async-done | bytes 98320 | tf_op jit(solution)/shard_map/psum | solution.py:215
  447.6 43.5 %reduce-scatter.14.cloned.1.call-done = bf16[96,1536]{1,0:T(8,128)(2,1)} async-done(((bf16[768,1536]{1,0:T(8,128)(2,1)}), bf16[96,1536]{1,0:T(8,128)(2,1)}) %reduce-scatter.14.cloned.1.call-update) | async-done | bytes 294928 | tf_op jit(solution)/shard_map/reduce_scatter | solution.py:206
  495.1 53.2 %reduce-scatter.10.cloned.1.call-done = bf16[192,2,768]{2,0,1:T(8,128)(2,1)} async-done(((bf16[1536,2,768]{2,0,1:T(8,128)(2,1)}), bf16[192,2,768]{2,0,1:T(8,128)(2,1)}) %reduce-scatter.10.cloned.1.call-update) | async-done | bytes 589840 | tf_op jit(solution)/shard_map/reduce_scatter | solution.py:197
  555.8 212.0 %all-gather.16.cloned.1.call-done = bf16[4096,1536]{1,0:T(8,128)(2,1)} async-done(((bf16[1024,1536]{1,0:T(8,128)(2,1)}), bf16[4096,1536]{1,0:T(8,128)(2,1)}) %all-gather.16.cloned.1.call-update) | async-done | bytes 12582928 | tf_op jit(solution)/shard_map/all_gather | solution.py:187
  767.9 8.7 reduce_sum.368
  781.6 47.2 %reduce-scatter.8.cloned.1.call-done = bf16[256,1536]{1,0:T(8,128)(2,1)} async-done(((bf16[1024,1536]{1,0:T(8,128)(2,1)}), bf16[256,1536]{1,0:T(8,128)(2,1)}) %reduce-scatter.8.cloned.1.call-update) | async-done | bytes 786448 | tf_op jit(solution)/shard_map/reduce_scatter | solution.py:135
  833.2 24.0 %all-reduce.29 = (bf16[1536]{0:T(1024)(128)(2,1)S(1)}, f32[6,768]{1,0:T(8,128)S(1)}, bf16[5,256]{1,0:T(8,128)(2,1)S(1)}, f32[3,12]{1,0:T(4,128)S(1)}) all-reduce(f32[1536]{0:T(1024)S(1)} %get-tuple-element.710, f32[6,768]{1,0:T(8,128)S(1)} %copy-done.28, ...), channel_id=1, replica_groups=mesh['dp'=8,'head'=4] {'dp'}, use_global_device_ids=true, to_apply=%region_31.32 | all-reduce | flops 7460 | bytes 54048 | tf_op jit(solution)/shard_map/psum | solution.py:211
  858.4 11.1 %all-reduce.30 = (bf16[1536]{0:T(1024)(128)(2,1)S(1)}, bf16[5,256]{1,0:T(8,128)(2,1)S(1)}) all-reduce(bf16[1536]{0:T(1024)(128)(2,1)S(1)} %get-tuple-element.664, bf16[5,256]{1,0:T(8,128)(2,1)S(1)} %get-tuple-element.666), channel_id=1, replica_groups=mesh['dp'=8,'head'=4] {'head'}, use_global_device_ids=true, to_apply=%region_32.33 | all-reduce | flops 2816 | bytes 11264 | tf_op jit(solution)/shard_map/psum | solution.py:217
  (458 shorter events, 220.1 us)
Async XLA Ops:
  7.3 68.6 %all-gather.8.cloned.1.call-start = ((), (), s32[]{:S(2)}) async-start(), calls=%async_computation.5 | async-start | bytes 3932160 | tf_op jit(solution)/shard_map/all_gather | solution.py:109
  8.0 107.8 %all-gather.10.cloned.1.call-start = ((), (), s32[]{:S(2)}) async-start(), calls=%async_computation.6 | async-start | bytes 5308416 | tf_op jit(solution)/shard_map/all_gather | solution.py:100
  10.6 181.7 %all-gather.12.cloned.1.call-start = ((), (), s32[]{:S(2)}) async-start(), calls=%async_computation.7 | async-start | bytes 2654208 | tf_op jit(solution)/shard_map/all_gather | solution.py:103
  11.4 200.9 %all-gather.14.cloned.1.call-start = ((), (), s32[]{:S(2)}) async-start(), calls=%async_computation.9 | async-start | bytes 3932160 | tf_op jit(solution)/shard_map/all_gather | solution.py:142
  12.0 358.8 %reduce-scatter.12.cloned.1.call-start = ((), (), s32[]{:S(2)}) async-start(), calls=%async_computation.11 | async-start | bytes 884736 | tf_op jit(solution)/shard_map/reduce_scatter | solution.py:203
  12.1 67.4 %copy-start.26 = (f32[1536]{0:T(1024)}, f32[1536]{0:T(1024)S(1)}, u32[]{:S(2)}) copy-start(f32[1536]{0:T(1024)S(1)} %convert_element_type.152) | copy-start | bytes 18436
  34.4 47.5 %copy-start.22 = (bf16[1536,12]{0,1:T(8,128)(2,1)}, bf16[1536,12]{0,1:T(8,128)(2,1)S(1)}, u32[]{:S(2)}) copy-start(bf16[1536,12]{0,1:T(8,128)(2,1)S(1)} %reshape.309) | copy-start | bytes 110596
  79.8 47.4 %copy-start = (bf16[1024,1536]{1,0:T(8,128)(2,1)}, bf16[1024,1536]{1,0:T(8,128)(2,1)S(1)}, u32[]{:S(2)}) copy-start(bf16[1024,1536]{1,0:T(8,128)(2,1)S(1)} %fusion.100) | copy-start | bytes 9437188
  336.8 82.7 %reduce-scatter.16.cloned.1.call-start = ((), (), s32[]{:S(2)}) async-start(), calls=%async_computation.15 | async-start | bytes 442368
  338.4 106.6 %all-reduce.33.cloned.1.call-start = ((), (), s32[]{:S(2)}) async-start(), calls=%async_computation.12 | async-start | bytes 196608 | tf_op jit(solution)/shard_map/psum | solution.py:215
  370.8 120.2 %reduce-scatter.14.cloned.1.call-start = ((), (), s32[]{:S(2)}) async-start(), calls=%async_computation.13 | async-start | bytes 2654208 | tf_op jit(solution)/shard_map/reduce_scatter | solution.py:206
  377.4 170.8 %reduce-scatter.10.cloned.1.call-start = ((), (), s32[]{:S(2)}) async-start(), calls=%async_computation.10 | async-start | bytes 5308416 | tf_op jit(solution)/shard_map/reduce_scatter | solution.py:197
  390.9 377.0 %all-gather.16.cloned.1.call-start = ((), (), s32[]{:S(2)}) async-start(), calls=%async_computation.14 | async-start | bytes 15728640 | tf_op jit(solution)/shard_map/all_gather | solution.py:187
  404.0 424.8 %reduce-scatter.8.cloned.1.call-start = ((), (), s32[]{:S(2)}) async-start(), calls=%async_computation.8 | async-start | bytes 3932160 | tf_op jit(solution)/shard_map/reduce_scatter | solution.py:135
  447.5 100.7 %copy-start.6 = (f32[192,2,768]{2,1,0:T(2,128)S(1)}, f32[192,2,768]{2,1,0:T(2,128)}, u32[]{:S(2)}) copy-start(f32[192,2,768]{2,1,0:T(2,128)} %param.27) | copy-start | bytes 3538948
  780.1 48.6 %copy-start.53 = (f32[256,1]{0,1:T(1,128)S(1)}, f32[256,1]{0,1:T(1,128)}, u32[]{:S(2)}) copy-start(f32[256,1]{0,1:T(1,128)} %constant_dynamic-slice_fusion.1) | copy-start | bytes 3076
  780.2 48.6 %copy-start.54 = (f32[256]{0:T(256)S(1)}, f32[256]{0:T(256)}, u32[]{:S(2)}) copy-start(f32[256]{0:T(256)} %dynamic-slice.6) | copy-start | bytes 3076
  828.8 40.7 %copy-start.46 = (f32[1,5,256]{2,0,1:T(1,128)S(1)}, f32[1,5,256]{2,0,1:T(1,128)}, u32[]{:S(2)}) copy-start(f32[1,5,256]{2,0,1:T(1,128)} %get-tuple-element.739) | copy-start | bytes 15364
  828.9 41.9 %copy-start.14 = (f32[5,768]{1,0:T(8,128)S(1)}, f32[5,768]{1,0:T(8,128)}, u32[]{:S(2)}) copy-start(f32[5,768]{1,0:T(8,128)} %copy-done.13) | copy-start | bytes 46084
  828.9 41.9 %copy-start.29 = (f32[1,6,768]{2,0,1:T(1,128)S(1)}, f32[1,6,768]{2,0,1:T(1,128)}, u32[]{:S(2)}) copy-start(f32[1,6,768]{2,0,1:T(1,128)} %get-tuple-element.729) | copy-start | bytes 55300
  828.9 41.9 %copy-start.30 = (f32[1,6,768]{2,0,1:T(1,128)S(1)}, f32[1,6,768]{2,0,1:T(1,128)}, u32[]{:S(2)}) copy-start(f32[1,6,768]{2,0,1:T(1,128)} %get-tuple-element.730) | copy-start | bytes 55300
  828.9 43.2 %copy-start.41 = (f32[1536]{0:T(1024)S(1)}, f32[1536]{0:T(1024)}, u32[]{:S(2)}) copy-start(f32[1536]{0:T(1024)} %get-tuple-element.612) | copy-start | bytes 18436
  828.9 43.2 %copy-start.42 = (f32[1536]{0:T(1024)S(1)}, f32[1536]{0:T(1024)}, u32[]{:S(2)}) copy-start(f32[1536]{0:T(1024)} %get-tuple-element.613) | copy-start | bytes 18436
  828.9 43.1 %copy-start.44 = (f32[1536]{0:T(1024)S(1)}, f32[1536]{0:T(1024)}, u32[]{:S(2)}) copy-start(f32[1536]{0:T(1024)} %param.26) | copy-start | bytes 18436
  (51 other events, 462.8 us)
Sparse Core Ops, SparseCore 0:
  9.6 66.1 all-gather.7
  78.3 37.4 all-gather.9
  118.2 28.8 all-gather.11
  148.6 63.6 all-gather.13
  336.9 33.8 reduce-scatter.11
  374.2 33.8 reduce-scatter.15
  410.5 34.4 all-reduce.32
  448.9 42.0 reduce-scatter.13
  494.5 53.7 reduce-scatter.9
  549.6 218.1 all-gather.15
  770.2 58.5 reduce-scatter.7
